TPU v7x, 32 devices: a whole 2x2x4 slice. The times are simulated.
32 devices in a mesh: depth: 8 (over z, core), freq: 4 (over y, x).
Axes of the slice: x: 2, y: 2, z: 4, core: 2. Of those that a mesh axis runs over, the one named last changes fastest.
Arguments:
- fields_top: bfloat16 [8, 2, 4, 2, 384, 384], P('depth', None, 'freq'), may hold values from -6 to 6
- surface: bfloat16 [2, 2, 4, 2, 384, 384], P(None, None, 'freq'), may hold values from -6 to 6
- up_state: bfloat16 [8, 4, 2, 384, 384], P('depth', 'freq'), may hold values from -6 to 6
- angular_freq: float32 [4], P('freq'), may hold values from 0.5 to 2.5
- class_slowness: float32 [8], replicated, may hold values from 0.6 to 1.3
- velocity_class: int32 [8, 12, 12], P('depth'), may hold values from 0 to 7
- slowness_detail: float32 [8, 384, 384], P('depth'), may hold values from 0.5 to 1.5
Outputs:
- reflectivity: bfloat16 [8, 384, 384], P('depth', 'freq')
- up_out: bfloat16 [8, 4, 2, 384, 384], P('depth', 'freq')
All inputs are finite; a program needn't handle non-finite values.
Results may differ from a plain program's by a relative error of at most 0.023.
Values may be sent and summed in bfloat16 or wider, within the bound.
A program may use at most 64 MiB of HBM per device.

v0:
```python
import jax
import jax.numpy as jnp
from jax import lax
from jax.sharding import PartitionSpec as P

LAYERS = 1
TICKS = 3
CLASSES = 8
BLOCK = 32


DEPTH_STEP = 1.0
EPSILON = 1e-06


def passed_along(block, axis, distance):
    devices = range(lax.axis_size(axis))
    route = [(i - distance, i) for i in devices if i - distance in devices]
    return lax.ppermute(block, axis, route)


def make_tables(lateral):
    positions = jnp.arange(lateral, dtype=jnp.int32)
    wrapped = positions[:, None] * positions[None, :] % lateral
    angles = wrapped.astype(jnp.float32) * (2.0 * jnp.pi / lateral)
    cosine_table = jnp.cos(angles).astype(jnp.bfloat16)
    sine_table = jnp.sin(angles).astype(jnp.bfloat16)
    folded = jnp.where(positions < lateral // 2, positions, positions - lateral)
    kappa = folded.astype(jnp.float32) * (2.0 * jnp.pi / lateral)
    wavenumber_sq = kappa[:, None] ** 2 + kappa[None, :] ** 2
    return (cosine_table, sine_table, wavenumber_sq)


def cell_slowness(velocity_class, class_slowness, slowness_detail):
    count, lateral = (slowness_detail.shape[0], slowness_detail.shape[1])
    blocks = lateral // BLOCK
    onehot = (velocity_class[..., None] == jnp.arange(CLASSES, dtype=jnp.int32)).astype(jnp.float32)
    block_slow = jnp.sum(onehot * class_slowness, axis=-1)
    spread = jnp.broadcast_to(
        block_slow[:, :, None, :, None], (count, blocks, BLOCK, blocks, BLOCK)
    )
    slowness = spread.reshape(count, lateral, lateral) * slowness_detail
    return (slowness, jnp.mean(slowness, axis=(1, 2)))


def propagate(
    real_part, imag_part, angular, slowness, reference_slow, cosine_table, sine_table, wavenumber_sq
):
    lateral = real_part.shape[0]
    joined_cols = jnp.concatenate([cosine_table, sine_table], axis=1)
    joined_rows = jnp.concatenate([cosine_table, sine_table], axis=0)
    product = jnp.dot(
        jnp.concatenate([real_part, imag_part], axis=0),
        joined_cols,
        preferred_element_type=jnp.float32,
    )
    real_cos, real_sin = (product[:lateral, :lateral], product[:lateral, lateral:])
    imag_cos, imag_sin = (product[lateral:, :lateral], product[lateral:, lateral:])
    half_real = (real_cos + imag_sin).astype(jnp.bfloat16)
    half_imag = (imag_cos - real_sin).astype(jnp.bfloat16)
    product = jnp.dot(
        joined_rows,
        jnp.concatenate([half_real, half_imag], axis=1),
        preferred_element_type=jnp.float32,
    )
    cos_real, cos_imag = (product[:lateral, :lateral], product[:lateral, lateral:])
    sin_real, sin_imag = (product[lateral:, :lateral], product[lateral:, lateral:])
    spec_real = cos_real + sin_imag
    spec_imag = cos_imag - sin_real
    vertical = (angular * reference_slow) ** 2 - wavenumber_sq
    travel = jnp.sqrt(jnp.maximum(vertical, 0.0)) * DEPTH_STEP
    decay = jnp.exp(-jnp.sqrt(jnp.maximum(-vertical, 0.0)) * DEPTH_STEP) / (lateral * lateral)
    phase_real = decay * jnp.cos(travel)
    phase_imag = decay * jnp.sin(travel)
    shifted_real = (spec_real * phase_real - spec_imag * phase_imag).astype(jnp.bfloat16)
    shifted_imag = (spec_real * phase_imag + spec_imag * phase_real).astype(jnp.bfloat16)
    product = jnp.dot(
        joined_rows,
        jnp.concatenate([shifted_real, shifted_imag], axis=1),
        preferred_element_type=jnp.float32,
    )
    cos_real, cos_imag = (product[:lateral, :lateral], product[:lateral, lateral:])
    sin_real, sin_imag = (product[lateral:, :lateral], product[lateral:, lateral:])
    back_real = (cos_real - sin_imag).astype(jnp.bfloat16)
    back_imag = (cos_imag + sin_real).astype(jnp.bfloat16)
    product = jnp.dot(
        jnp.concatenate([back_real, back_imag], axis=0),
        joined_cols,
        preferred_element_type=jnp.float32,
    )
    real_cos, real_sin = (product[:lateral, :lateral], product[:lateral, lateral:])
    imag_cos, imag_sin = (product[lateral:, :lateral], product[lateral:, lateral:])
    space_real = real_cos - imag_sin
    space_imag = imag_cos + real_sin
    lens = angular * DEPTH_STEP * (slowness - reference_slow)
    lens_cos, lens_sin = (jnp.cos(lens), jnp.sin(lens))
    new_real = (space_real * lens_cos - space_imag * lens_sin).astype(jnp.bfloat16)
    new_imag = (space_real * lens_sin + space_imag * lens_cos).astype(jnp.bfloat16)
    return (new_real, new_imag)


def advance(fields, angular, slowness, reference_slow, tables):
    cosine_table, sine_table, wavenumber_sq = tables

    def single(real_part, imag_part, frequency):
        return propagate(
            real_part,
            imag_part,
            frequency,
            slowness,
            reference_slow,
            cosine_table,
            sine_table,
            wavenumber_sq,
        )

    new_real, new_imag = jax.vmap(single)(fields[:, 0], fields[:, 1], angular)
    return jnp.stack([new_real, new_imag], axis=1)


def advance_pair(fields, angular, slowness, reference_slow, tables):

    def one_field(member):
        return advance(member, angular, slowness, reference_slow, tables)

    return jax.vmap(one_field)(fields)


def image_terms(fields):
    source = fields[0].astype(jnp.float32)
    receiver = fields[1].astype(jnp.float32)
    image_part = jnp.sum(source[:, 0] * receiver[:, 0] + source[:, 1] * receiver[:, 1], axis=0)
    illum_part = jnp.sum(source[:, 0] * source[:, 0] + source[:, 1] * source[:, 1], axis=0)
    return (image_part, illum_part)


def per_device(
    fields_top, surface, up_state, angular_freq, class_slowness, velocity_class, slowness_detail
):
    lateral = fields_top.shape[-1]
    tables = make_tables(lateral)
    slowness, reference_slow = cell_slowness(velocity_class, class_slowness, slowness_detail)
    segment_index = lax.axis_index("depth")
    image_sum = [jnp.zeros((lateral, lateral), jnp.float32)]
    illumination = [jnp.zeros((lateral, lateral), jnp.float32)]
    sources = [None] * LAYERS
    fields = fields_top[0]
    for turn_index in range(TICKS):
        layer_index = 0
        fields = advance_pair(
            fields, angular_freq, slowness[layer_index], reference_slow[layer_index], tables
        )
        image_part, illum_part = image_terms(fields)
        image_sum[layer_index] = image_sum[layer_index] + image_part
        illumination[layer_index] = illumination[layer_index] + illum_part
        if turn_index == TICKS - 1:
            sources[layer_index] = fields[0]
        if turn_index + 1 < TICKS:
            from_above = passed_along(fields, "depth", 1)
            fields = jnp.where(segment_index == 0, surface[turn_index], from_above)
    image_all = jnp.stack(image_sum)
    illum_all = jnp.stack(illumination)
    image_total, illum_total = (
        lax.psum(image_all.astype(jnp.bfloat16), "freq").astype(jnp.float32),
        lax.psum(illum_all.astype(jnp.bfloat16), "freq").astype(jnp.float32),
    )
    damping = jnp.mean(illum_total, axis=(1, 2))
    balanced = image_total / (illum_total + damping[:, None, None])
    mean_square = jnp.mean(balanced * balanced, axis=(1, 2))
    reflect = (balanced * lax.rsqrt(mean_square + EPSILON)[:, None, None]).astype(jnp.bfloat16)
    row_count = lateral // lax.axis_size("freq")
    reflect_part = lax.dynamic_slice_in_dim(
        reflect, lax.axis_index("freq") * row_count, row_count, 1
    )
    rising_wave = passed_along(up_state[0], "depth", -1)
    for layer_index in reversed(range(LAYERS)):
        scattered = reflect[layer_index].astype(jnp.float32)[None, None] * sources[
            layer_index
        ].astype(jnp.float32)
        rising_wave = (rising_wave.astype(jnp.float32) + scattered).astype(jnp.bfloat16)
        rising_wave = advance(
            rising_wave, angular_freq, slowness[layer_index], reference_slow[layer_index], tables
        )
    return (reflect_part, rising_wave[None])


def solution(mesh):
    return jax.shard_map(
        per_device,
        mesh=mesh,
        in_specs=(
            P("depth", None, "freq", None, None, None),
            P(None, None, "freq", None, None, None),
            P("depth", "freq", None, None, None),
            P("freq"),
            P(),
            P("depth", None, None),
            P("depth", None, None),
        ),
        out_specs=(P("depth", "freq", None), P("depth", "freq", None, None, None)),
        check_vma=False,
    )
```

profile of v0, /device:TPU:0, one launch (start us, length us, event | category | flops | bytes accessed | tf_op | source)
XLA Modules:
  0.0 157.0 jit_solution(17389596648066102286)
XLA Ops:
  7.2 2.6 %sine_convert_fusion = (bf16[384,384]{0,1:T(8,128)(2,1)S(1)}, bf16[384,384]{0,1:T(8,128)(2,1)S(1)}) fusion(), kind=kLoop, calls=%fused_computation.237 | loop fusion | flops 1622016 | bytes 589824 | tf_op jit(solution)/shard_map/convert_element_type | solution.py:27
  9.8 0.7 copy.102
  10.5 0.7 select_reduce_fusion
  11.2 1.9 %broadcast_in_dim.6 = f32[12,32,12,32]{3,2,1,0:T(8,128)} broadcast(f32[12,12]{1,0:T(8,128)S(1)} %select_reduce_fusion), dimensions={0,2} | broadcast | bytes 590400 | tf_op jit(solution)/shard_map/broadcast_in_dim | solution.py:39
  13.1 2.5 %broadcast_in_dim.7 = f32[1,384,384]{2,1,0:T(8,128)S(1)} reshape(f32[12,32,12,32]{3,2,1,0:T(8,128)} %broadcast_in_dim.6) | data formatting | bytes 1179648 | tf_op jit(solution)/shard_map/broadcast_in_dim | solution.py:39
  16.4 0.8 fusion.140
  18.1 1.4 convolution_bitcast_fusion.11
  19.5 0.3 fusion.11
  19.8 2.6 %cosine_multiply_fusion.1 = (f32[384,384]{0,1:T(8,128)S(1)}, f32[384,384]{0,1:T(8,128)S(1)}) fusion(f32[384]{0:T(512)S(1)} %fusion.123, f32[]{:T(128)} %bitcast.11), kind=kLoop, calls=%fused_computation.233 | loop fusion | flops 1327104 | bytes 1181188 | tf_op jit(solution)/shard_map/vmap(vmap())/mul | solution.py:73
  22.3 1.4 convolution_bitcast_fusion.10
  23.7 0.4 fusion.41
  24.1 1.4 convolution_bitcast_fusion.9
  25.8 2.3 %fusion.113 = (f32[384,384]{1,0:T(8,128)S(1)}, f32[384,384]{1,0:T(8,128)S(1)}) fusion(f32[1,384,384]{2,1,0:T(8,128)S(1)} %get-tuple-element.7, f32[]{:T(128)} %div.22, f32[]{:T(128)} %bitcast.257), kind=kLoop, calls=%fused_computation.245 | loop fusion | flops 294912 | bytes 1769480 | tf_op jit(solution)/shard_map/vmap(vmap())/mul | solution.py:97
  28.1 1.4 convolution_bitcast_fusion.8
  29.6 0.4 fusion.43
  30.0 1.2 pad_maximum_fusion
  31.2 3.4 %collective-permute-start = (bf16[2,1,2,384,384]{4,3,0,2,1:T(8,128)(2,1)}, bf16[2,1,2,384,384]{4,3,0,2,1:T(8,128)(2,1)}, u32[]{:S(2)}, u32[]{:S(2)}) collective-permute-start(bf16[2,1,2,384,384]{4,3,0,2,1:T(8,128)(2,1)} %pad_maximum_fusion), channel_id=1, source_target_pairs={{0,4},{4,8},{8,12},{12,16},{16,20},{20,24},{24,28},{1,5},{5,9},{9,... | collective-permute-start | bytes 3538952 | tf_op jit(solution)/shard_map/ppermute | solution.py:19
  34.6 1.9 %fusion.141 = (bf16[1,2,1,2,384,384]{5,4,3,2,1,0:T(8,128)(2,1)S(1)}, bf16[1,2,1,2,384,384]{5,4,3,2,1,0:T(8,128)(2,1)S(1)}) fusion(bf16[2,2,1,2,384,384]{5,4,3,2,1,0:T(8,128)(2,1)} %param.8), kind=kLoop, calls=%fused_computation.281 | loop fusion | bytes 4718592 | tf_op jit(solution)/shard_map/slice | solution.py:160
  36.8 1.4 convolution_bitcast_fusion.7
  38.2 0.3 fusion.7
  38.5 1.4 convolution_bitcast_fusion.6
  39.9 0.4 fusion.45
  40.3 1.4 convolution_bitcast_fusion.5
  42.0 1.4 convolution_bitcast_fusion.4
  43.4 0.4 fusion.47
  44.0 16.8 %collective-permute-start.1 = (bf16[2,1,2,384,384]{4,3,0,2,1:T(8,128)(2,1)S(1)}, bf16[2,1,2,384,384]{4,3,0,2,1:T(8,128)(2,1)S(1)}, u32[]{:S(2)}, u32[]{:S(2)}) collective-permute-start(bf16[2,1,2,384,384]{4,3,0,2,1:T(8,128)(2,1)S(1)} %pad_maximum_fusion.1), channel_id=1, source_target_pairs={{0,4},{4,8},{8,12},{12,16},{16,20},{20,24},{24,28},{1,5},{5,9},{9,... | collective-permute-start | bytes 3538952 | tf_op jit(solution)/shard_map/ppermute | solution.py:19
  61.1 1.8 %collective-permute-done.1 = bf16[2,1,2,384,384]{4,3,0,2,1:T(8,128)(2,1)S(1)} collective-permute-done((bf16[2,1,2,384,384]{4,3,0,2,1:T(8,128)(2,1)S(1)}, bf16[2,1,2,384,384]{4,3,0,2,1:T(8,128)(2,1)S(1)}, u32[]{:S(2)}, u32[]{:S(2)}) %collective-permute-start.1) | collective-permute-done | bytes 1179680 | tf_op jit(solution)/shard_map/ppermute | solution.py:19
  63.2 1.4 convolution_bitcast_fusion.3
  64.9 1.4 convolution_bitcast_fusion.2
  66.3 0.4 fusion.49
  66.7 1.4 convolution_bitcast_fusion.1
  68.4 1.4 convolution_bitcast_fusion
  69.8 0.4 fusion.52
  70.4 1.3 fusion.120
  71.7 1.6 collective-permute-start.2
  73.3 59.8 %all-reduce.3.cloned.1.call-done = (bf16[1,384,384]{2,1,0:T(8,128)(2,1)}, bf16[1,384,384]{2,1,0:T(8,128)(2,1)}) async-done(((bf16[1,384,384]{2,1,0:T(8,128)(2,1)}, bf16[1,384,384]{2,1,0:T(8,128)(2,1)}), (bf16[1,384,384]{2,1,0:T(8,128)(2,1)}, bf16[1,384,384]{2,1,0:T(8,128)(2,1)})) %all-reduce.3.cloned.1.call-update) | async-done | bytes 589840 | tf_op jit(solution)/shard_map/psum | solution.py:165
  133.1 1.7 %convert_reduce_fusion = f32[]{:T(128)} fusion(bf16[1,384,384]{2,1,0:T(8,128)(2,1)} %get-tuple-element.2), kind=kLoop, calls=%fused_computation.120 | loop fusion | flops 294911 | bytes 294916 | tf_op jit(solution)/shard_map/reduce_sum | solution.py:167
  135.5 1.8 %multiply_reduce_fusion = f32[]{:T(128)} fusion(f32[]{:T(128)S(6)} %div.25, bf16[1,384,384]{2,1,0:T(8,128)(2,1)} %get-tuple-element.2, bf16[1,384,384]{2,1,0:T(8,128)(2,1)} %get-tuple-element.3), kind=kLoop, calls=%fused_computation.229 | loop fusion | flops 884735 | bytes 589832 | tf_op jit(solution)/shard_map/reduce_sum | solution.py:169
  138.0 1.2 bitcast_convert_fusion
  139.5 0.8 convolution_bitcast_fusion.15
  140.4 0.8 convolution_bitcast_fusion.12
  141.1 3.1 %subtract_convert_fusion.7 = (bf16[1,384,384]{1,2,0:T(8,128)(2,1)S(1)}, bf16[1,384,384]{1,2,0:T(8,128)(2,1)S(1)}) fusion(f32[384]{0:T(512)S(1)} %fusion.123, f32[]{:T(128)} %bitcast.11, f32[768,1,768]{0,2,1:T(8,128)S(1)} %convolution_bitcast_fusion.12), kind=kLoop, calls=%fused_computation.222 | loop fusion | flops 2801664 | bytes 2953220 | tf_op jit(solution)/shard_map/vmap()/convert_element_type | solution.py:75
  144.3 0.8 convolution_bitcast_fusion.14
  145.2 0.6 constant_dynamic-slice_fusion
  145.9 0.8 convolution_bitcast_fusion.13
  146.7 0.3 copy-done.3
  146.9 2.3 %fusion.117 = (bf16[1,1,384,384]{3,2,1,0:T(8,128)(2,1)S(1)}, bf16[1,1,384,384]{3,2,1,0:T(8,128)(2,1)S(1)}) fusion(f32[1,384,384]{2,1,0:T(8,128)S(1)} %copy-done.3, f32[]{:T(128)} %div.22, f32[]{:T(128)} %bitcast.258, f32[1,768,768]{2,1,0:T(8,128)S(1)} %convolution_bitcast_fusion.13), kind=kLoop, calls=%fused_computation.252 | loop fusion | flops 1769472 | bytes 3538952 | tf_op jit(solution)/shard_map/stack | solution.py:118
  149.3 0.9 maximum_bitcast_fusion.32
  (36 shorter events, 3.0 us)
Async XLA Ops:
  7.2 125.9 %all-reduce.3.cloned.1.call-start = ((), (), s32[]{:S(2)}) async-start(), calls=%async_computation | async-start | bytes 1179648 | tf_op jit(solution)/shard_map/psum | solution.py:165
  13.1 3.3 %copy-start.5 = (f32[1,384,384]{2,1,0:T(8,128)S(1)}, f32[1,384,384]{2,1,0:T(8,128)}, u32[]{:S(2)}) copy-start(f32[1,384,384]{2,1,0:T(8,128)} %param.13) | copy-start | bytes 1769476
  15.6 2.2 %copy-start.4 = (bf16[1,2,1,2,384,384]{5,4,3,2,1,0:T(8,128)(2,1)S(1)}, bf16[1,2,1,2,384,384]{5,4,3,2,1,0:T(8,128)(2,1)}, u32[]{:S(2)}) copy-start(bf16[1,2,1,2,384,384]{5,4,3,2,1,0:T(8,128)(2,1)} %param.7) | copy-start | bytes 3538948
  17.1 8.7 %copy-start.2 = (f32[1,384,384]{2,1,0:T(8,128)}, f32[1,384,384]{2,1,0:T(8,128)S(1)}, u32[]{:S(2)}) copy-start(f32[1,384,384]{2,1,0:T(8,128)S(1)} %get-tuple-element.7) | copy-start | bytes 1769476
  30.0 1.2 copy-start
  31.2 5.3 %collective-permute-start = (bf16[2,1,2,384,384]{4,3,0,2,1:T(8,128)(2,1)}, bf16[2,1,2,384,384]{4,3,0,2,1:T(8,128)(2,1)}, u32[]{:S(2)}, u32[]{:S(2)}) collective-permute-start(bf16[2,1,2,384,384]{4,3,0,2,1:T(8,128)(2,1)} %pad_maximum_fusion), channel_id=1, source_target_pairs={{0,4},{4,8},{8,12},{12,16},{16,20},{20,24},{24,28},{1,5},{5,9},{9,... | collective-permute-start | bytes 3538952 | tf_op jit(solution)/shard_map/ppermute | solution.py:19
  43.8 17.0 %copy-start.1 = (bf16[2,1,1,384,384]{4,3,0,2,1:T(8,128)(2,1)S(1)}, bf16[2,1,1,384,384]{4,3,0,2,1:T(8,128)(2,1)}, u32[]{:S(2)}) copy-start(bf16[2,1,1,384,384]{4,3,0,2,1:T(8,128)(2,1)} %copy-done) | copy-start | bytes 1769476
  44.0 19.0 %collective-permute-start.1 = (bf16[2,1,2,384,384]{4,3,0,2,1:T(8,128)(2,1)S(1)}, bf16[2,1,2,384,384]{4,3,0,2,1:T(8,128)(2,1)S(1)}, u32[]{:S(2)}, u32[]{:S(2)}) collective-permute-start(bf16[2,1,2,384,384]{4,3,0,2,1:T(8,128)(2,1)S(1)} %pad_maximum_fusion.1), channel_id=1, source_target_pairs={{0,4},{4,8},{8,12},{12,16},{16,20},{20,24},{24,28},{1,5},{5,9},{9,... | collective-permute-start | bytes 3538952 | tf_op jit(solution)/shard_map/ppermute | solution.py:19
  70.4 1.3 copy-start.6
  71.7 67.5 %collective-permute-start.2 = (bf16[1,2,384,384]{3,2,1,0:T(8,128)(2,1)S(1)}, bf16[1,2,384,384]{3,2,1,0:T(8,128)(2,1)S(1)}, u32[]{:S(2)}, u32[]{:S(2)}) collective-permute-start(bf16[1,2,384,384]{3,2,1,0:T(8,128)(2,1)S(1)} %bitcast.261), channel_id=1, source_target_pairs={{4,0},{8,4},{12,8},{16,12},{20,16},{24,20},{28,24},{5,1},{9,5},{13... | collective-permute-start | bytes 1769480 | tf_op jit(solution)/shard_map/ppermute | solution.py:19
  145.9 1.1 copy-start.3
Sparse Core Ops, SparseCore 0:
  71.8 61.2 all-reduce.2
where the time goes:
time: 157 us
  waiting for transfers between devices  61.7 us (39%)
  other arithmetic  27.7 us (18%)
  starting transfers between devices  21.8 us (14%)
  matrix products  20.2 us (13%)
  between operations  17.2 us (11%)
  local copies, waits for them, and re-layouts  8.43 us (5%)
    psum x1, waiting for transfers between devices, per_device(): lax.psum(illum_all.astype(jnp.bfloat16), 'freq').astype(jnp.float32)  59.8 us
    ppermute x3, starting transfers between devices, passed_along(): return lax.ppermute(block, axis, route)  21.8 us
    dot_general x4, matrix products, propagate(): jnp.dot(joined_rows, jnp.concatenate([shifted_real, shifted_imag], axis=1...  5.13 us
    dot_general x4, matrix products, propagate(): jnp.dot(jnp.concatenate([back_real, back_imag], axis=0), joined_cols, pre...  5.05 us
    dot_general x4, matrix products, propagate(): jnp.dot(jnp.concatenate([real_part, imag_part], axis=0), joined_cols, pre...  5.05 us
    dot_general x4, matrix products, propagate(): jnp.dot(joined_rows, jnp.concatenate([half_real, half_imag], axis=1), pre...  4.96 us
    another operation x6, other arithmetic, advance(): return jnp.stack([new_real, new_imag], axis=1)  4.86 us
    broadcast_in_dim x2, local copies, waits for them, and re-layouts, cell_slowness(): jnp.broadcast_to(block_slow[:, :, None, :, None], (count, blocks, BLOCK,...  4.38 us
  transfers between devices with their start and end apart: 4, of which 2 were waited for; matrix products, arithmetic and copies ran while one was open for 4% of the time, Pallas kernels for 0%

commit v1 on v0

v1 whole, which is shorter than its diff:
```python
import functools

import jax
import jax.numpy as jnp
import numpy as np
from jax import lax
from jax.experimental import pallas as pl
from jax.experimental.pallas import tpu as pltpu
from jax.sharding import PartitionSpec as P

TICKS = 3
EPSILON = 1e-06
F32 = jnp.float32
BF16 = jnp.bfloat16
MESH = pl.DeviceIdType.MESH
PAD = 16


def cos_sin(angle):
    turns = jnp.floor(angle * (0.5 / np.pi) + 0.5)
    half = (angle - turns * (2.0 * np.pi)) * 0.5
    sq = half * half
    s = 1.0 / 6227020800.0
    for c in (-1.0 / 39916800, 1.0 / 362880, -1.0 / 5040, 1.0 / 120, -1.0 / 6, 1.0):
        s = s * sq + c
    s = s * half
    k = 1.0 / 479001600
    for c in (-1.0 / 3628800, 1.0 / 40320, -1.0 / 720, 1.0 / 24, -0.5, 1.0):
        k = k * sq + c
    return 1.0 - 2.0 * s * s, 2.0 * s * k


def kernel(
    sizes, ang, classes, top, surface, up_in, vc, detail, cos_t, sin_t,
    refl_out, up_out,
    wmat, lmat, cur, half, shifted, back, kept, params, packed, surf, rising, far_src,
    imgs, gathered, zsend, zrecv, total0, bal,
    surf_sem, up_sem, pk_send, pk_recv, src_sem, rs_send, rs_recv, z_send, z_recv, ag_send, ag_recv,
):
    n, nd, nf, blocks, ncls = sizes
    d, f = lax.axis_index("depth"), lax.axis_index("freq")
    rows = n // nf
    step_rows = n // blocks
    w = ang[0]

    def at(shift):
        return (lax.rem(d + shift + nd, nd), f)

    def peer(k):
        return lax.rem(f + k, nf)

    def up_copy():
        return pltpu.make_async_remote_copy(
            src_ref=up_in, dst_ref=rising, send_sem=up_sem.at[0], recv_sem=up_sem.at[1],
            device_id=at(-1), device_id_type=MESH)

    def pk_copy(t):
        return pltpu.make_async_remote_copy(
            src_ref=packed.at[0], dst_ref=packed.at[t], send_sem=pk_send.at[t],
            recv_sem=pk_recv.at[t], device_id=at(-t), device_id_type=MESH)

    def src_copy():
        return pltpu.make_async_remote_copy(
            src_ref=kept.at[TICKS - 1], dst_ref=far_src, send_sem=src_sem.at[0],
            recv_sem=src_sem.at[1], device_id=at(TICKS - 1), device_id_type=MESH)

    def rs_copy(t, k):
        return pltpu.make_async_remote_copy(
            src_ref=imgs.at[t, peer(k)], dst_ref=gathered.at[t, k], send_sem=rs_send.at[t, k],
            recv_sem=rs_recv.at[t, k], device_id=(d, peer(k)), device_id_type=MESH)

    def z_copy(t):
        return pltpu.make_async_remote_copy(
            src_ref=zsend.at[t], dst_ref=zrecv.at[t], send_sem=z_send.at[t],
            recv_sem=z_recv.at[t], device_id=at(t), device_id_type=MESH)

    def ag_copy(k):
        return pltpu.make_async_remote_copy(
            src_ref=bal.at[0], dst_ref=bal.at[k], send_sem=ag_send.at[k],
            recv_sem=ag_recv.at[k], device_id=(d, peer(k)), device_id_type=MESH)

    surf_copy = pltpu.make_async_copy(
        surface.at[jnp.minimum(nd - 1 - d, TICKS - 2)],
        surf, surf_sem.at[0])

    @pl.when(d >= nd - (TICKS - 1))
    def _():
        surf_copy.start()

    barrier = pltpu.get_barrier_semaphore()
    shifts = [s for s in range(-(TICKS - 1), TICKS) if s != 0]
    for s in shifts:
        pl.semaphore_signal(barrier, inc=1, device_id=at(s), device_id_type=MESH)
    for k in range(1, nf):
        pl.semaphore_signal(barrier, inc=1, device_id=(d, peer(k)), device_id_type=MESH)

    def slow_rows(i):
        ids = vc[i : i + 1, :]
        val = jnp.zeros((1, n), F32)
        for c in range(ncls):
            val = val + jnp.where(ids == c, classes[c], 0.0)
        return val * detail[i * step_rows : (i + 1) * step_rows, :]

    acc = jnp.zeros((step_rows, n), F32)
    for i in range(blocks):
        acc = acc + slow_rows(i)
    ref_own = jnp.sum(acc, keepdims=True) * (1.0 / (n * n))
    for i in range(blocks):
        packed[0, i * step_rows : (i + 1) * step_rows, :] = (slow_rows(i) - ref_own).astype(BF16)
    hi = ref_own.astype(BF16)
    lo = (ref_own - hi.astype(F32)).astype(BF16)
    packed[0, n : n + PAD, :] = jnp.broadcast_to(hi, (PAD, n))
    packed[0, n + PAD : n + 2 * PAD, :] = jnp.broadcast_to(lo, (PAD, n))

    pl.semaphore_wait(barrier, len(shifts) + nf - 1)
    for t in range(1, TICKS):
        pk_copy(t).start()

    @pl.when(d > 0)
    def _():
        up_copy().start()

    c, s = cos_t[...], sin_t[...]
    wmat[:n, :n] = c
    wmat[n:, n:] = c
    wmat[:n, n:] = -s
    wmat[n:, :n] = s
    lmat[:n, :n] = c
    lmat[n:, n:] = c
    lmat[:n, n:] = s
    lmat[n:, :n] = -s

    chunk = 32

    def make_params(t):
        ref = packed[t, n : n + 1, 0:1].astype(F32) + packed[t, n + PAD : n + PAD + 1, 0:1].astype(F32)
        limit = (w * ref) * (w * ref)
        col = lax.broadcasted_iota(jnp.int32, (1, n), 1)
        kcol = jnp.where(col < n // 2, col, col - n).astype(F32) * (2.0 * np.pi / n)
        kcol = kcol * kcol

        def body(i, _):
            off = pl.multiple_of(i * chunk, chunk)
            row = lax.broadcasted_iota(jnp.int32, (chunk, 1), 0) + off
            krow = jnp.where(row < n // 2, row, row - n).astype(F32) * (2.0 * np.pi / n)
            q = limit - (krow * krow + kcol)
            root = jnp.sqrt(jnp.abs(q))
            decay = jnp.where(q < 0.0, jnp.exp(-root), 1.0) * (1.0 / (n * n))
            pc, ps = cos_sin(jnp.where(q > 0.0, root, 0.0))
            params[t, 0, pl.ds(off, chunk), :] = decay * pc
            params[t, 1, pl.ds(off, chunk), :] = decay * ps
            lc, ls = cos_sin(w * packed[t, pl.ds(off, chunk), :].astype(F32))
            params[t, 2, pl.ds(off, chunk), :] = lc
            params[t, 3, pl.ds(off, chunk), :] = ls
            return 0

        lax.fori_loop(0, n // chunk, body, 0)

    def load(ref, member):
        cur[:, :n] = ref[member, 0]
        cur[:, n:] = ref[member, 1]

    def reduce_tick(t):
        for k in range(1, nf):
            rs_copy(t, k).wait()
        tot = imgs[t, f].astype(F32)
        for k in range(1, nf):
            tot = tot + gathered[t, k].astype(F32)
        return tot

    def run_step(j, _):
        tick = lax.rem(j, TICKS)

        for t in range(TICKS):
            @pl.when(j == t)
            def _():
                if t > 0:
                    pk_copy(t).wait()
                make_params(t)

        for m in range(2):
            @pl.when(j == m * TICKS)
            def _():
                load(top, m)

        for t in range(1, TICKS):
            for m in range(2):
                @pl.when((j == m * TICKS + t) & (d == nd - t))
                def _():
                    if m == 0:
                        surf_copy.wait()
                    load(surf, m)

        @pl.when(j == 2 * TICKS)
        def _():
            tot2 = reduce_tick(TICKS - 1)
            zsend[TICKS - 1] = tot2.astype(BF16)
            z_copy(TICKS - 1).start()
            z_copy(1).wait()
            part = total0[...] + zrecv[1].astype(F32)
            z_copy(TICKS - 1).wait()
            part = part + zrecv[TICKS - 1].astype(F32)
            damp = part[2 * rows : 2 * rows + 1, 0:1]
            bal[0] = (part[:rows] / (part[rows : 2 * rows] + damp)).astype(BF16)
            for k in range(1, nf):
                ag_copy(k).start()
            sq = bal[0].astype(F32)
            sq = sq * sq
            for k in range(1, nf):
                ag_copy(k).wait()
                v = bal[k].astype(F32)
                sq = sq + v * v
            mean_sq = jnp.sum(sq, keepdims=True) * (1.0 / (n * n))
            scale = lax.rsqrt(mean_sq + EPSILON)
            refl_out[...] = (bal[0].astype(F32) * scale).astype(BF16)
            src_copy().wait()

            @pl.when(d < nd - 1)
            def _():
                up_copy().wait_recv()

            @pl.when(d == nd - 1)
            def _():
                rising[...] = jnp.zeros_like(rising)

            @pl.when(d > 0)
            def _():
                up_copy().wait_send()

            for k in range(nf):
                owner = lax.rem(f + nf - k, nf)
                off = pl.multiple_of(owner * rows, rows)
                r = (bal[k].astype(F32) * scale).astype(BF16).astype(F32)
                for part_i in range(2):
                    lanes = slice(part_i * n, (part_i + 1) * n)
                    cur[pl.ds(off, rows), lanes] = (
                        rising[part_i, pl.ds(off, rows), :].astype(F32)
                        + r * far_src[pl.ds(off, rows), lanes].astype(F32)
                    ).astype(BF16)

        slot = jnp.where(j == 2 * TICKS, 0, tick)

        res = jnp.dot(cur[...], wmat[...], preferred_element_type=F32)
        half[:n, :] = res[:, :n].astype(BF16)
        half[n:, :] = res[:, n:].astype(BF16)
        v = jnp.dot(lmat[...], half[...], preferred_element_type=F32)
        vr, vi = v[:n], v[n:]
        hr, hm = params[slot, 0], params[slot, 1]
        shifted[:n, :] = (vr * hr - vi * hm).astype(BF16)
        shifted[n:, :] = (vr * hm + vi * hr).astype(BF16)
        x = jnp.dot(wmat[...], shifted[...], preferred_element_type=F32)
        back[:, :n] = x[:n].astype(BF16)
        back[:, n:] = x[n:].astype(BF16)
        y = jnp.dot(back[...], lmat[...], preferred_element_type=F32)
        yr, yi = y[:, :n], y[:, n:]
        lc, ls = params[slot, 2], params[slot, 3]
        cur[:, :n] = (yr * lc - yi * ls).astype(BF16)
        cur[:, n:] = (yr * ls + yi * lc).astype(BF16)

        for t in range(TICKS):
            @pl.when(j == t)
            def _():
                kept[t] = cur[...]
                if t == TICKS - 1:
                    src_copy().start()

            @pl.when(j == TICKS + t)
            def _():
                acc_i = jnp.zeros((1, n), F32)
                for g in range(nf):
                    rs = slice(g * rows, (g + 1) * rows)
                    sr, si = kept[t, rs, :n].astype(F32), kept[t, rs, n:].astype(F32)
                    rr, ri = cur[rs, :n].astype(F32), cur[rs, n:].astype(F32)
                    ill = sr * sr + si * si
                    imgs[t, g, :rows, :] = (sr * rr + si * ri).astype(BF16)
                    imgs[t, g, rows : 2 * rows, :] = ill.astype(BF16)
                    acc_i = acc_i + jnp.sum(ill, axis=0, keepdims=True)
                mean_i = jnp.sum(acc_i, keepdims=True) * (1.0 / (n * n))
                for g in range(nf):
                    imgs[t, g, 2 * rows :, :] = jnp.broadcast_to(mean_i, (PAD, n)).astype(BF16)
                for k in range(1, nf):
                    rs_copy(t, k).start()
                if t == 1:
                    total0[...] = reduce_tick(0)
                if t == TICKS - 1:
                    zsend[1] = reduce_tick(1).astype(BF16)
                    z_copy(1).start()

        return 0

    lax.fori_loop(0, 2 * TICKS + 1, run_step, 0)
    up_out[0] = cur[:, :n]
    up_out[1] = cur[:, n:]


def per_device(fields_top, surface, up_state, angular_freq, class_slowness, velocity_class, slowness_detail):
    n = fields_top.shape[-1]
    nd, nf = lax.axis_size("depth"), lax.axis_size("freq")
    blocks = velocity_class.shape[-1]
    ncls = class_slowness.shape[0]
    rows = n // nf
    vc = jnp.repeat(velocity_class[0], n // blocks, axis=1)
    pos = np.arange(n)
    ang = (pos[:, None] * pos[None, :] % n) * (2.0 * np.pi / n)
    cos_t = jnp.asarray(np.cos(ang).astype(np.float32)).astype(BF16)
    sin_t = jnp.asarray(np.sin(ang).astype(np.float32)).astype(BF16)
    vmem = pl.BlockSpec(memory_space=pltpu.VMEM)
    smem = pl.BlockSpec(memory_space=pltpu.SMEM)
    V = pltpu.VMEM
    DMA = pltpu.SemaphoreType.DMA
    blk = 2 * rows + PAD
    refl, up = pl.pallas_call(
        functools.partial(kernel, (n, nd, nf, blocks, ncls)),
        out_shape=(
            jax.ShapeDtypeStruct((rows, n), BF16),
            jax.ShapeDtypeStruct((2, n, n), BF16),
        ),
        in_specs=[smem, smem, vmem, pl.BlockSpec(memory_space=pl.ANY), vmem, vmem, vmem, vmem, vmem],
        out_specs=(vmem, vmem),
        scratch_shapes=[
            V((2 * n, 2 * n), BF16), V((2 * n, 2 * n), BF16),
            V((n, 2 * n), BF16), V((2 * n, n), BF16), V((2 * n, n), BF16), V((n, 2 * n), BF16),
            V((TICKS, n, 2 * n), BF16), V((TICKS, 4, n, n), F32),
            V((TICKS, n + 2 * PAD, n), BF16), V((2, 2, n, n), BF16),
            V((2, n, n), BF16), V((n, 2 * n), BF16),
            V((TICKS, nf, blk, n), BF16), V((TICKS, nf, blk, n), BF16),
            V((TICKS, blk, n), BF16), V((TICKS, blk, n), BF16), V((blk, n), F32),
            V((nf, rows, n), BF16),
            DMA((1,)), DMA((2,)), DMA((TICKS,)), DMA((TICKS,)), DMA((2,)),
            DMA((TICKS, nf)), DMA((TICKS, nf)), DMA((TICKS,)), DMA((TICKS,)), DMA((nf,)), DMA((nf,)),
        ],
        compiler_params=pltpu.CompilerParams(
            collective_id=0, has_side_effects=True, vmem_limit_bytes=60 * 1024 * 1024
        ),
        name="window",
    )(
        angular_freq, class_slowness, fields_top[0, :, 0], surface[:, :, 0], up_state[0, 0], vc,
        slowness_detail[0], cos_t, sin_t,
    )
    return refl[None], up[None, None]


def solution(mesh):
    return jax.shard_map(
        per_device,
        mesh=mesh,
        in_specs=(
            P("depth", None, "freq", None, None, None),
            P(None, None, "freq", None, None, None),
            P("depth", "freq", None, None, None),
            P("freq"),
            P(),
            P("depth", None, None),
            P("depth", None, None),
        ),
        out_specs=(P("depth", "freq", None), P("depth", "freq", None, None, None)),
        check_vma=False,
    )
```

time: 157 us -> 74 us (0.47)
  Pallas kernels: 0 us -> 67.4 us
  waiting for transfers between devices: 61.7 us -> 0 us
  other arithmetic: 27.7 us -> 0 us
  starting transfers between devices: 21.8 us -> 0 us
  matrix products: 20.2 us -> 0 us
  between operations: 17.2 us -> 1.29 us
  local copies, waits for them, and re-layouts: 8.43 us -> 4.94 us
    pallas_call x0 -> x1, Pallas kernels: none -> 67.4 us  [per_device(): pl.pallas_call(functools.partial(kernel, (n, nd, nf, blocks, ncls)), out_...]
    psum x1 -> x0, waiting for transfers between devices: 59.8 us -> none  [per_device(): lax.psum(illum_all.astype(jnp.bfloat16), 'freq').astype(jnp.float32)]
    ppermute x3 -> x0, starting transfers between devices: 21.8 us -> none  [passed_along(): return lax.ppermute(block, axis, route)]
    dot_general x16 -> x0, matrix products: 20.2 us -> none  [the longest x4 5.13 us: propagate(): jnp.dot(joined_rows, jnp.concatenate([shifted_real, shifted_imag], axis=1...]
    convert_element_type x14 -> x0, other arithmetic: 9.59 us -> none  [the longest x4 4.28 us: propagate(): (spec_real * phase_real - spec_imag * phase_imag).astype(jnp.bfloat16)]
    reduce_sum x4 -> x0, other arithmetic: 5.03 us -> none  [the longest x1 1.82 us: per_device(): mean_square = jnp.mean(balanced * balanced, axis=(1, 2))]
    mul x2 -> x0, other arithmetic: 4.87 us -> none  [the longest x1 2.56 us: propagate(): phase_real = decay * jnp.cos(travel)]
    another operation x6 -> x0, other arithmetic: 4.86 us -> none  [advance(): return jnp.stack([new_real, new_imag], axis=1)]
  transfers between devices with their start and end apart: 4 -> 0, of which waited for: 2 -> 0; matrix products, arithmetic and copies ran while one was open for 4% -> 0% of each run, Pallas kernels for 0% -> 0%
where the time goes in v1:
time: 74 us; the launch traced here: 73.7 us
  Pallas kernels  67.4 us (91%)
  local copies, waits for them, and re-layouts  4.94 us (7%)
  between operations  1.29 us (2%)
    pallas_call x1, Pallas kernels, per_device(): pl.pallas_call(functools.partial(kernel, (n, nd, nf, blocks, ncls)), out_...  67.4 us
    unnamed x3, local copies, waits for them, and re-layouts  4.16 us

profile of v1, /device:TPU:0, one launch (start us, length us, event | category | flops | bytes accessed | tf_op | source)
XLA Modules:
  0.0 73.7 jit_solution(14635195665416304313)
XLA Ops:
  1.3 0.7 copy.13
  2.0 0.1 broadcast_in_dim.9
  2.1 0.7 reshape.7.vc
  2.8 67.4 %window.1 = (bf16[96,384]{1,0:T(8,128)(2,1)}, bf16[2,384,384]{2,1,0:T(8,128)(2,1)}) custom-call(f32[1]{0:T(128)S(6)} %copy.16.ang, f32[8]{0:T(128)} %classes.1, bf16[2,2,384,384]{3,2,1,0:T(8,128)(2,1)} %bitcast.10, bf16[2,2,2,384,384]{4,3,2,1,0:T(8,128)(2,1)} %bitcast.9, bf16[2,384,384]{2,1,0:T(8,128)(2,1)} %bitcast.11, s32[12,384]{1,0:T(8,128)} %reshape.7.vc, ...), custom_call_target="tpu_custom_call" | custom-call | tf_op jit(solution)/shard_map/window/pallas_call | solution.py:312
  70.2 1.5 %copy.17 = bf16[1,96,384]{2,1,0:T(8,128)(2,1)} copy(bf16[1,96,384]{2,1,0:T(8,128)(2,1)} %bitcast.14) | data formatting | bytes 147456
  71.7 1.9 %copy.18 = bf16[1,1,2,384,384]{4,3,2,1,0:T(8,128)(2,1)} copy(bf16[1,1,2,384,384]{4,3,2,1,0:T(8,128)(2,1)} %bitcast.13) | data formatting | bytes 1179648

commit v2 on v1

--- a/solution.py
+++ b/solution.py
@@ -34,8 +34,8 @@
     sizes, ang, classes, top, surface, up_in, vc, detail, cos_t, sin_t,
     refl_out, up_out,
     wmat, lmat, cur, half, shifted, back, kept, params, packed, surf, rising, far_src,
-    imgs, gathered, zsend, zrecv, total0, bal,
-    surf_sem, up_sem, pk_send, pk_recv, src_sem, rs_send, rs_recv, z_send, z_recv, ag_send, ag_recv,
+    imgs, gathered, xrecv, zsend, zrecv, total0, bal, rstate,
+    surf_sem, up_sem, pk_send, pk_recv, src_sem, rs_send, rs_recv, z_sem, x_sem, ag_send, ag_recv,
 ):
     n, nd, nf, blocks, ncls = sizes
     d, f = lax.axis_index("depth"), lax.axis_index("freq")
@@ -54,10 +54,13 @@
             src_ref=up_in, dst_ref=rising, send_sem=up_sem.at[0], recv_sem=up_sem.at[1],
             device_id=at(-1), device_id_type=MESH)
 
-    def pk_copy(t):
-        return pltpu.make_async_remote_copy(
-            src_ref=packed.at[0], dst_ref=packed.at[t], send_sem=pk_send.at[t],
-            recv_sem=pk_recv.at[t], device_id=at(-t), device_id_type=MESH)
+    odd = lax.rem(d, 2) == 1
+    even = lax.rem(d, 2) == 0
+
+    def pk_copy(src, dst, shift):
+        return pltpu.make_async_remote_copy(
+            src_ref=packed.at[src], dst_ref=packed.at[dst], send_sem=pk_send.at[src, dst],
+            recv_sem=pk_recv.at[dst], device_id=at(shift), device_id_type=MESH)
 
     def src_copy():
         return pltpu.make_async_remote_copy(
@@ -66,13 +69,19 @@
 
     def rs_copy(t, k):
         return pltpu.make_async_remote_copy(
-            src_ref=imgs.at[t, peer(k)], dst_ref=gathered.at[t, k], send_sem=rs_send.at[t, k],
-            recv_sem=rs_recv.at[t, k], device_id=(d, peer(k)), device_id_type=MESH)
-
-    def z_copy(t):
-        return pltpu.make_async_remote_copy(
-            src_ref=zsend.at[t], dst_ref=zrecv.at[t], send_sem=z_send.at[t],
-            recv_sem=z_recv.at[t], device_id=at(t), device_id_type=MESH)
+            src_ref=imgs.at[t, peer(k)], dst_ref=gathered.at[t // 2, k],
+            send_sem=rs_send.at[t // 2, k], recv_sem=rs_recv.at[t // 2, k],
+            device_id=(d, peer(k)), device_id_type=MESH)
+
+    def x_copy():
+        return pltpu.make_async_remote_copy(
+            src_ref=imgs.at[1], dst_ref=xrecv, send_sem=x_sem.at[0], recv_sem=x_sem.at[1],
+            device_id=(d + 1 - 2 * lax.rem(d, 2), f), device_id_type=MESH)
+
+    def z_copy():
+        return pltpu.make_async_remote_copy(
+            src_ref=zsend, dst_ref=zrecv, send_sem=z_sem.at[0], recv_sem=z_sem.at[1],
+            device_id=at(TICKS - 1), device_id_type=MESH)
 
     def ag_copy(k):
         return pltpu.make_async_remote_copy(
@@ -94,11 +103,17 @@
     for k in range(1, nf):
         pl.semaphore_signal(barrier, inc=1, device_id=(d, peer(k)), device_id_type=MESH)
 
+    ids = vc[...]
+    block_val = jnp.zeros(ids.shape, F32)
+    for c in range(ncls):
+        block_val = block_val + jnp.where(ids == c, classes[c], 0.0)
+    col_id = lax.broadcasted_iota(jnp.int32, (1, n), 1)
+
     def slow_rows(i):
-        ids = vc[i : i + 1, :]
         val = jnp.zeros((1, n), F32)
-        for c in range(ncls):
-            val = val + jnp.where(ids == c, classes[c], 0.0)
+        for b in range(blocks):
+            inside = (col_id >= b * step_rows) & (col_id < (b + 1) * step_rows)
+            val = jnp.where(inside, block_val[i : i + 1, b : b + 1], val)
         return val * detail[i * step_rows : (i + 1) * step_rows, :]
 
     acc = jnp.zeros((step_rows, n), F32)
@@ -109,16 +124,15 @@
         packed[0, i * step_rows : (i + 1) * step_rows, :] = (slow_rows(i) - ref_own).astype(BF16)
     hi = ref_own.astype(BF16)
     lo = (ref_own - hi.astype(F32)).astype(BF16)
-    packed[0, n : n + PAD, :] = jnp.broadcast_to(hi, (PAD, n))
-    packed[0, n + PAD : n + 2 * PAD, :] = jnp.broadcast_to(lo, (PAD, n))
+    packed[0, n:, :128] = jnp.broadcast_to(hi, (PAD, 128))
+    packed[0, n:, 128:] = jnp.broadcast_to(lo, (PAD, n - 128))
 
     pl.semaphore_wait(barrier, len(shifts) + nf - 1)
-    for t in range(1, TICKS):
-        pk_copy(t).start()
-
-    @pl.when(d > 0)
+    pk_copy(0, 1, -1).start()
+
+    @pl.when(odd)
     def _():
-        up_copy().start()
+        pk_copy(0, 2, -2).start()
 
     c, s = cos_t[...], sin_t[...]
     wmat[:n, :n] = c
@@ -133,7 +147,7 @@
     chunk = 32
 
     def make_params(t):
-        ref = packed[t, n : n + 1, 0:1].astype(F32) + packed[t, n + PAD : n + PAD + 1, 0:1].astype(F32)
+        ref = packed[t, n : n + 1, 0:1].astype(F32) + packed[t, n : n + 1, 128:129].astype(F32)
         limit = (w * ref) * (w * ref)
         col = lax.broadcasted_iota(jnp.int32, (1, n), 1)
         kcol = jnp.where(col < n // 2, col, col - n).astype(F32) * (2.0 * np.pi / n)
@@ -165,27 +179,71 @@
             rs_copy(t, k).wait()
         tot = imgs[t, f].astype(F32)
         for k in range(1, nf):
-            tot = tot + gathered[t, k].astype(F32)
+            tot = tot + gathered[t // 2, k].astype(F32)
         return tot
 
+    def start_rs(t):
+        for k in range(1, nf):
+            rs_copy(t, k).start()
+
+    def add_partner(t):
+        x_copy().wait()
+        for g in range(nf):
+            imgs[t, g] = (imgs[t, g].astype(F32) + xrecv[g].astype(F32)).astype(BF16)
+        start_rs(t)
+
     def run_step(j, _):
-        tick = lax.rem(j, TICKS)
-
-        for t in range(TICKS):
-            @pl.when(j == t)
-            def _():
-                if t > 0:
-                    pk_copy(t).wait()
-                make_params(t)
+        @pl.when(j == 0)
+        def _():
+            make_params(0)
+
+        @pl.when(j == 2)
+        def _():
+            pk_copy(0, 1, -1).wait()
+
+            @pl.when(odd)
+            def _():
+                pk_copy(1, 2, -1).start()
+
+            make_params(1)
+
+        @pl.when(j == 4)
+        def _():
+            @pl.when(odd)
+            def _():
+                pk_copy(0, 2, -2).wait()
+                pk_copy(1, 2, -1).wait_send()
+
+            @pl.when(even)
+            def _():
+                pk_copy(1, 2, -1).wait_recv()
+
+            @pl.when(d > 0)
+            def _():
+                up_copy().start()
+
+            make_params(2)
+
+        @pl.when((j == 5) & odd)
+        def _():
+            add_partner(0)
 
         for m in range(2):
-            @pl.when(j == m * TICKS)
+            @pl.when(j == m)
             def _():
                 load(top, m)
 
         for t in range(1, TICKS):
+            @pl.when(j == 2 * t)
+            def _():
+                cur[...] = kept[t - 1]
+
+            @pl.when(j == 2 * t + 1)
+            def _():
+                cur[...] = rstate[...]
+
             for m in range(2):
-                @pl.when((j == m * TICKS + t) & (d == nd - t))
+                @pl.when((j == 2 * t + m) & (d == nd - t))
                 def _():
                     if m == 0:
                         surf_copy.wait()
@@ -193,13 +251,11 @@
 
         @pl.when(j == 2 * TICKS)
         def _():
-            tot2 = reduce_tick(TICKS - 1)
-            zsend[TICKS - 1] = tot2.astype(BF16)
-            z_copy(TICKS - 1).start()
-            z_copy(1).wait()
-            part = total0[...] + zrecv[1].astype(F32)
-            z_copy(TICKS - 1).wait()
-            part = part + zrecv[TICKS - 1].astype(F32)
+            zsend[...] = reduce_tick(2).astype(BF16)
+            z_copy().start()
+            total0[...] = reduce_tick(0)
+            z_copy().wait()
+            part = total0[...] + zrecv[...].astype(F32)
             damp = part[2 * rows : 2 * rows + 1, 0:1]
             bal[0] = (part[:rows] / (part[rows : 2 * rows] + damp)).astype(BF16)
             for k in range(1, nf):
@@ -238,7 +294,7 @@
                         + r * far_src[pl.ds(off, rows), lanes].astype(F32)
                     ).astype(BF16)
 
-        slot = jnp.where(j == 2 * TICKS, 0, tick)
+        slot = jnp.where(j == 2 * TICKS, 0, j // 2)
 
         res = jnp.dot(cur[...], wmat[...], preferred_element_type=F32)
         half[:n, :] = res[:, :n].astype(BF16)
@@ -258,14 +314,16 @@
         cur[:, n:] = (yr * ls + yi * lc).astype(BF16)
 
         for t in range(TICKS):
-            @pl.when(j == t)
+            @pl.when(j == 2 * t)
             def _():
                 kept[t] = cur[...]
                 if t == TICKS - 1:
                     src_copy().start()
 
-            @pl.when(j == TICKS + t)
-            def _():
+            @pl.when(j == 2 * t + 1)
+            def _():
+                if t < TICKS - 1:
+                    rstate[...] = cur[...]
                 acc_i = jnp.zeros((1, n), F32)
                 for g in range(nf):
                     rs = slice(g * rows, (g + 1) * rows)
@@ -278,13 +336,20 @@
                 mean_i = jnp.sum(acc_i, keepdims=True) * (1.0 / (n * n))
                 for g in range(nf):
                     imgs[t, g, 2 * rows :, :] = jnp.broadcast_to(mean_i, (PAD, n)).astype(BF16)
-                for k in range(1, nf):
-                    rs_copy(t, k).start()
+                if t == 0:
+                    @pl.when(even)
+                    def _():
+                        start_rs(0)
                 if t == 1:
-                    total0[...] = reduce_tick(0)
-                if t == TICKS - 1:
-                    zsend[1] = reduce_tick(1).astype(BF16)
-                    z_copy(1).start()
+                    x_copy().start()
+                if t == 2:
+                    @pl.when(even)
+                    def _():
+                        add_partner(2)
+
+                    @pl.when(odd)
+                    def _():
+                        start_rs(2)
 
         return 0
 
@@ -299,7 +364,7 @@
     blocks = velocity_class.shape[-1]
     ncls = class_slowness.shape[0]
     rows = n // nf
-    vc = jnp.repeat(velocity_class[0], n // blocks, axis=1)
+    vc = velocity_class[0]
     pos = np.arange(n)
     ang = (pos[:, None] * pos[None, :] % n) * (2.0 * np.pi / n)
     cos_t = jnp.asarray(np.cos(ang).astype(np.float32)).astype(BF16)
@@ -321,13 +386,13 @@
             V((2 * n, 2 * n), BF16), V((2 * n, 2 * n), BF16),
             V((n, 2 * n), BF16), V((2 * n, n), BF16), V((2 * n, n), BF16), V((n, 2 * n), BF16),
             V((TICKS, n, 2 * n), BF16), V((TICKS, 4, n, n), F32),
-            V((TICKS, n + 2 * PAD, n), BF16), V((2, 2, n, n), BF16),
+            V((TICKS, n + PAD, n), BF16), V((2, 2, n, n), BF16),
             V((2, n, n), BF16), V((n, 2 * n), BF16),
-            V((TICKS, nf, blk, n), BF16), V((TICKS, nf, blk, n), BF16),
-            V((TICKS, blk, n), BF16), V((TICKS, blk, n), BF16), V((blk, n), F32),
-            V((nf, rows, n), BF16),
-            DMA((1,)), DMA((2,)), DMA((TICKS,)), DMA((TICKS,)), DMA((2,)),
-            DMA((TICKS, nf)), DMA((TICKS, nf)), DMA((TICKS,)), DMA((TICKS,)), DMA((nf,)), DMA((nf,)),
+            V((TICKS, nf, blk, n), BF16), V((2, nf, blk, n), BF16), V((nf, blk, n), BF16),
+            V((blk, n), BF16), V((blk, n), BF16), V((blk, n), F32),
+            V((nf, rows, n), BF16), V((n, 2 * n), BF16),
+            DMA((1,)), DMA((2,)), DMA((2, TICKS)), DMA((TICKS,)), DMA((2,)),
+            DMA((2, nf)), DMA((2, nf)), DMA((2,)), DMA((2,)), DMA((nf,)), DMA((nf,)),
         ],
         compiler_params=pltpu.CompilerParams(
             collective_id=0, has_side_effects=True, vmem_limit_bytes=60 * 1024 * 1024

time: 74 us -> 64.9 us (0.88)
  Pallas kernels: 67.4 us -> 58.5 us
    pallas_call x1, Pallas kernels: 67.4 us -> 58.5 us  [per_device(): pl.pallas_call(functools.partial(kernel, (n, nd, nf, blocks, ncls)), out_...]
where the time goes in v2:
time: 64.9 us; the launch traced here: 64.6 us
  Pallas kernels  58.5 us (90%)
  local copies, waits for them, and re-layouts  4.75 us (7%)
  between operations  1.29 us (2%)
    pallas_call x1, Pallas kernels, per_device(): pl.pallas_call(functools.partial(kernel, (n, nd, nf, blocks, ncls)), out_...  58.5 us
    unnamed x3, local copies, waits for them, and re-layouts  4.75 us

profile of v2, /device:TPU:0, one launch (start us, length us, event | category | flops | bytes accessed | tf_op | source)
XLA Modules:
  0.0 64.6 jit_solution(10742646957677316276)
XLA Ops:
  1.3 1.3 %copy.13 = s32[1,12,12]{2,1,0:T(8,128)} copy(s32[1,12,12]{2,0,1:T(1,128)} %param.14) | data formatting | bytes 1152
  2.6 58.5 %window.1 = (bf16[96,384]{1,0:T(8,128)(2,1)}, bf16[2,384,384]{2,1,0:T(8,128)(2,1)}) custom-call(f32[1]{0:T(128)S(6)} %copy.16.ang, f32[8]{0:T(128)} %classes.1, bf16[2,2,384,384]{3,2,1,0:T(8,128)(2,1)} %bitcast.10, bf16[2,2,2,384,384]{4,3,2,1,0:T(8,128)(2,1)} %bitcast.9, bf16[2,384,384]{2,1,0:T(8,128)(2,1)} %bitcast.11, s32[12,12]{1,0:T(8,128)} %bitcast.15, ...), custom_call_target="tpu_custom_call" | custom-call | tf_op jit(solution)/shard_map/window/pallas_call | solution.py:377
  61.1 1.5 %copy.17 = bf16[1,96,384]{2,1,0:T(8,128)(2,1)} copy(bf16[1,96,384]{2,1,0:T(8,128)(2,1)} %bitcast.14) | data formatting | bytes 147456
  62.6 1.9 %copy.18 = bf16[1,1,2,384,384]{4,3,2,1,0:T(8,128)(2,1)} copy(bf16[1,1,2,384,384]{4,3,2,1,0:T(8,128)(2,1)} %bitcast.13) | data formatting | bytes 1179648

commit v3 on v2

--- a/solution.py
+++ b/solution.py
@@ -224,9 +224,9 @@
 
             make_params(2)
 
-        @pl.when((j == 5) & odd)
-        def _():
-            add_partner(0)
+            @pl.when(odd)
+            def _():
+                add_partner(0)
 
         for m in range(2):
             @pl.when(j == m)

time: 64.9 us -> 64.7 us (level)
  no operation moved by 1% of the time
where the time goes in v3:
time: 64.7 us; the launch traced here: 64.4 us
  Pallas kernels  58.4 us (90%)
  local copies, waits for them, and re-layouts  4.75 us (7%)
  between operations  1.29 us (2%)
    pallas_call x1, Pallas kernels, per_device(): pl.pallas_call(functools.partial(kernel, (n, nd, nf, blocks, ncls)), out_...  58.4 us
    unnamed x3, local copies, waits for them, and re-layouts  4.75 us

profile of v3, /device:TPU:0, one launch (start us, length us, event | category | flops | bytes accessed | tf_op | source)
XLA Modules:
  0.0 64.4 jit_solution(13425594901634700369)
XLA Ops:
  1.3 1.3 %copy.13 = s32[1,12,12]{2,1,0:T(8,128)} copy(s32[1,12,12]{2,0,1:T(1,128)} %param.14) | data formatting | bytes 1152
  2.6 58.4 %window.1 = (bf16[96,384]{1,0:T(8,128)(2,1)}, bf16[2,384,384]{2,1,0:T(8,128)(2,1)}) custom-call(f32[1]{0:T(128)S(6)} %copy.16.ang, f32[8]{0:T(128)} %classes.1, bf16[2,2,384,384]{3,2,1,0:T(8,128)(2,1)} %bitcast.10, bf16[2,2,2,384,384]{4,3,2,1,0:T(8,128)(2,1)} %bitcast.9, bf16[2,384,384]{2,1,0:T(8,128)(2,1)} %bitcast.11, s32[12,12]{1,0:T(8,128)} %bitcast.15, ...), custom_call_target="tpu_custom_call" | custom-call | tf_op jit(solution)/shard_map/window/pallas_call | solution.py:377
  61.0 1.5 %copy.17 = bf16[1,96,384]{2,1,0:T(8,128)(2,1)} copy(bf16[1,96,384]{2,1,0:T(8,128)(2,1)} %bitcast.14) | data formatting | bytes 147456
  62.5 1.9 %copy.18 = bf16[1,1,2,384,384]{4,3,2,1,0:T(8,128)(2,1)} copy(bf16[1,1,2,384,384]{4,3,2,1,0:T(8,128)(2,1)} %bitcast.13) | data formatting | bytes 1179648

commit v4 on v3

--- a/solution.py
+++ b/solution.py
@@ -222,11 +222,11 @@
             def _():
                 up_copy().start()
 
+            @pl.when(odd)
+            def _():
+                add_partner(0)
+
             make_params(2)
-
-            @pl.when(odd)
-            def _():
-                add_partner(0)
 
         for m in range(2):
             @pl.when(j == m)

time: 64.7 us -> 65.4 us (1.011)
  Pallas kernels: 58.4 us -> 59.1 us
    pallas_call x1, Pallas kernels: 58.4 us -> 59.1 us  [per_device(): pl.pallas_call(functools.partial(kernel, (n, nd, nf, blocks, ncls)), out_...]
where the time goes in v4:
time: 65.4 us; the launch traced here: 65.1 us
  Pallas kernels  59.1 us (90%)
  local copies, waits for them, and re-layouts  4.75 us (7%)
  between operations  1.29 us (2%)
    pallas_call x1, Pallas kernels, per_device(): pl.pallas_call(functools.partial(kernel, (n, nd, nf, blocks, ncls)), out_...  59.1 us
    unnamed x3, local copies, waits for them, and re-layouts  4.75 us

profile of v4, /device:TPU:0, one launch (start us, length us, event | category | flops | bytes accessed | tf_op | source)
XLA Modules:
  0.0 65.1 jit_solution(1500784922001733302)
XLA Ops:
  1.3 1.3 %copy.13 = s32[1,12,12]{2,1,0:T(8,128)} copy(s32[1,12,12]{2,0,1:T(1,128)} %param.14) | data formatting | bytes 1152
  2.6 59.1 %window.1 = (bf16[96,384]{1,0:T(8,128)(2,1)}, bf16[2,384,384]{2,1,0:T(8,128)(2,1)}) custom-call(f32[1]{0:T(128)S(6)} %copy.16.ang, f32[8]{0:T(128)} %classes.1, bf16[2,2,384,384]{3,2,1,0:T(8,128)(2,1)} %bitcast.10, bf16[2,2,2,384,384]{4,3,2,1,0:T(8,128)(2,1)} %bitcast.9, bf16[2,384,384]{2,1,0:T(8,128)(2,1)} %bitcast.11, s32[12,12]{1,0:T(8,128)} %bitcast.15, ...), custom_call_target="tpu_custom_call" | custom-call | tf_op jit(solution)/shard_map/window/pallas_call | solution.py:377
  61.7 1.5 %copy.17 = bf16[1,96,384]{2,1,0:T(8,128)(2,1)} copy(bf16[1,96,384]{2,1,0:T(8,128)(2,1)} %bitcast.14) | data formatting | bytes 147456
  63.2 1.9 %copy.18 = bf16[1,1,2,384,384]{4,3,2,1,0:T(8,128)(2,1)} copy(bf16[1,1,2,384,384]{4,3,2,1,0:T(8,128)(2,1)} %bitcast.13) | data formatting | bytes 1179648
